TPU v7x, 32 devices: a whole 2x2x4 slice. The times are simulated.
32 devices in a mesh: shard: 4 (over z), ctx: 2 (over core), tp: 4 (over y, x).
Axes of the slice: x: 2, y: 2, z: 4, core: 2. Of those that a mesh axis runs over, the one named last changes fastest.
Arguments:
- tokens: bfloat16 [8, 1024, 768], P('shard', 'ctx'), may hold values from -6 to 6
- time_embed: float32 [8, 768], P('shard'), may hold values from -3 to 3
- segments: int32 [8, 1024], P('shard'), may hold values from 0 to 3, never falling along the last dimension, each value on 1 to 800 neighbouring positions
- w_qkv: bfloat16 [768, 3, 768], P('shard', None, 'tp'), may hold values from -0.21875 to 0.21875
- w_out: bfloat16 [768, 768], P('tp', 'shard'), may hold values from -0.875 to 0.875
- w_up: bfloat16 [768, 3072], P('shard', 'tp'), may hold values from -0.21875 to 0.21875
- w_down: bfloat16 [3072, 768], P('tp', 'shard'), may hold values from -0.21875 to 0.21875
- qv_bias: float32 [2, 768], P(None, 'tp'), may hold values from -0.625 to 0.625
- up_bias: float32 [3072], P('tp'), may hold values from -1.75 to 1.75
- norm_gains: float32 [2, 768], replicated, may hold values from 0.5 to 1.5
- norm_shifts: float32 [2, 768], replicated, may hold values from -1.75 to 1.75
- branch_bias: float32 [2, 768], replicated, may hold values from -1.75 to 1.75
- out_grad: bfloat16 [8, 1024, 768], P('shard', 'ctx'), may hold values from -8 to 8
Outputs:
- layer_out: float32 [8, 1024, 768], P('shard', 'ctx')
- input_grad: float32 [8, 1024, 768], P('shard', 'ctx')
- w_qkv_grad: float32 [768, 3, 768], P('shard', None, 'tp')
- w_out_grad: float32 [768, 768], P('tp', 'shard')
- w_up_grad: float32 [768, 3072], P('shard', 'tp')
- w_down_grad: float32 [3072, 768], P('tp', 'shard')
- qv_bias_grad: float32 [2, 768], P(None, 'tp')
- up_bias_grad: float32 [3072], P('tp')
- norm_gains_grad: float32 [2, 768], replicated
- norm_shifts_grad: float32 [2, 768], replicated
- branch_bias_grad: float32 [2, 768], replicated
Inputs may be any that keep to these rules, and one draw needn't show every extreme that they name: `segments`: document numbers never fall along a sequence; each document holds 1 to 800 tokens, and one of each sequence exactly 800.
All inputs are finite; a program needn't handle non-finite values.
Results may differ from a plain program's by a relative error of at most 0.018.
Values may be sent and summed in bfloat16 or wider, within the bound.
No kernel may reach another device: no remote copies, remote signals or barrier semaphores. Data moves between devices by JAX's collectives and lax.ppermute only.
A program may use at most 128 MiB of HBM per device.

v0:
```python
import jax
import jax.numpy as jnp
from jax import lax
from jax.sharding import PartitionSpec as P

HD = 64


def layer_norm(residual, gain_vec, shift_vec):
    center = residual - jnp.mean(residual, axis=-1, keepdims=True)
    spread = jnp.mean(center * center, axis=-1, keepdims=True)
    return center * lax.rsqrt(spread + 1e-05) * gain_vec + shift_vec


def exact_gelu(values):
    return jax.nn.gelu(values, approximate=False)


def fetch_weights(w_qkv, w_out, w_up, w_down):
    return (
        lax.all_gather(w_qkv, "shard", axis=0, tiled=True),
        lax.all_gather(w_out, "shard", axis=1, tiled=True),
        lax.all_gather(w_up, "shard", axis=0, tiled=True),
        lax.all_gather(w_down, "shard", axis=1, tiled=True),
    )


def across_heads(term_rows):
    return lax.psum(term_rows, "tp")


def masked_scores(query_blk, key_blk, labels_query, labels_key):
    query_len = query_blk.shape[0]
    key_len = key_blk.shape[0]
    head_count = query_blk.shape[1] // HD
    query_heads = query_blk.reshape(query_len, head_count, HD)
    key_heads = key_blk.reshape(key_len, head_count, HD)
    scores = jnp.einsum(
        "qhe,khe->hqk", query_heads, key_heads, preferred_element_type=jnp.float32
    ) * HD ** (-0.5)
    same_doc = labels_query[:, None] == labels_key[None, :]
    return jnp.where(same_doc[None], scores, -1e30)


def attend_forward(packed):
    query_blk, key_blk, value_blk, labels_query, labels_key = packed
    query_len = query_blk.shape[0]
    key_len = key_blk.shape[0]
    head_count = query_blk.shape[1] // HD
    scores = masked_scores(query_blk, key_blk, labels_query, labels_key)
    row_max = jnp.max(scores, axis=-1, keepdims=True)
    exp_scores = jnp.exp(scores - row_max)
    row_total = jnp.sum(exp_scores, axis=-1, keepdims=True)
    attn_probs = exp_scores / row_total
    value_heads = value_blk.reshape(key_len, head_count, HD)
    heads_out = jnp.einsum(
        "hqk,khe->qhe",
        attn_probs.astype(jnp.bfloat16),
        value_heads,
        preferred_element_type=jnp.float32,
    )
    return (heads_out.reshape(query_len, head_count * HD), (row_max + jnp.log(row_total))[..., 0])


def attend_backward(packed):
    query_blk, key_blk, value_blk, labels_query, labels_key, grad_blk, log_total = packed
    query_len = query_blk.shape[0]
    key_len = key_blk.shape[0]
    head_count = query_blk.shape[1] // HD
    scores = masked_scores(query_blk, key_blk, labels_query, labels_key)
    attn_probs = jnp.exp(scores - log_total[..., None])
    query_heads = query_blk.reshape(query_len, head_count, HD)
    key_heads = key_blk.reshape(key_len, head_count, HD)
    value_heads = value_blk.reshape(key_len, head_count, HD)
    grad_heads = grad_blk.reshape(query_len, head_count, HD)
    grad_probs = jnp.einsum(
        "qhe,khe->hqk", grad_heads, value_heads, preferred_element_type=jnp.float32
    )
    inner_sum = jnp.sum(attn_probs * grad_probs, axis=-1, keepdims=True)
    grad_scores = (attn_probs * (grad_probs - inner_sum)).astype(jnp.bfloat16)
    grad_query = jnp.einsum(
        "hqk,khe->qhe", grad_scores, key_heads, preferred_element_type=jnp.float32
    ) * HD ** (-0.5)
    grad_key = jnp.einsum(
        "hqk,qhe->khe", grad_scores, query_heads, preferred_element_type=jnp.float32
    ) * HD ** (-0.5)
    grad_value = jnp.einsum(
        "hqk,qhe->khe",
        attn_probs.astype(jnp.bfloat16),
        grad_heads,
        preferred_element_type=jnp.float32,
    )
    return (
        grad_query.reshape(query_len, head_count * HD),
        grad_key.reshape(key_len, head_count * HD),
        grad_value.reshape(key_len, head_count * HD),
    )


def shards(
    tokens,
    time_embed,
    segments,
    w_qkv,
    w_out,
    w_up,
    w_down,
    qv_bias,
    up_bias,
    norm_gains,
    norm_shifts,
    branch_bias,
    out_grad,
):
    seq_count, half_len, model_width = tokens.shape
    row_count = seq_count * half_len
    ctx_index = lax.axis_index("ctx")
    labels_query = lax.dynamic_slice_in_dim(segments, ctx_index * half_len, half_len, 1)
    stream_in = (tokens.astype(jnp.float32) + time_embed[:, None, :]).reshape(
        row_count, model_width
    )
    stream_low = stream_in.astype(jnp.bfloat16)
    cotangent = out_grad.astype(jnp.float32).reshape(row_count, model_width)
    full_qkv, full_out, full_up, full_down = fetch_weights(w_qkv, w_out, w_up, w_down)
    head_cols = full_qkv.shape[2]
    product = jnp.dot(
        stream_low, full_qkv.reshape(model_width, 3 * head_cols), preferred_element_type=jnp.float32
    ).reshape(row_count, 3, head_cols)
    query_low = (
        (product[:, 0] + qv_bias[0]).astype(jnp.bfloat16).reshape(seq_count, half_len, head_cols)
    )
    key_low = product[:, 1].astype(jnp.bfloat16).reshape(seq_count, half_len, head_cols)
    value_low = (
        (product[:, 2] + qv_bias[1]).astype(jnp.bfloat16).reshape(seq_count, half_len, head_cols)
    )
    key_all, value_all = (
        lax.all_gather(key_low, "ctx", axis=1, tiled=True),
        lax.all_gather(value_low, "ctx", axis=1, tiled=True),
    )
    heads_out, log_total = lax.map(
        attend_forward, (query_low, key_all, value_all, labels_query, segments)
    )
    heads_low = heads_out.reshape(row_count, head_cols).astype(jnp.bfloat16)
    attn_part = jnp.dot(heads_low, full_out, preferred_element_type=jnp.float32)
    attn_out = across_heads(attn_part) + branch_bias[0]
    normed, first_pullback = jax.vjp(
        layer_norm, stream_in + attn_out, norm_gains[0], norm_shifts[0]
    )
    normed_low = normed.astype(jnp.bfloat16)
    pre_act = jnp.dot(normed_low, full_up, preferred_element_type=jnp.float32) + up_bias
    activated, gelu_pullback = jax.vjp(exact_gelu, pre_act)
    act_low = activated.astype(jnp.bfloat16)
    down_part = jnp.dot(act_low, full_down, preferred_element_type=jnp.float32)
    ffn_out = across_heads(down_part) + branch_bias[1]
    layer_rows, second_pullback = jax.vjp(
        layer_norm, normed + ffn_out, norm_gains[1], norm_shifts[1]
    )
    back_qkv, back_out, back_up, back_down = fetch_weights(w_qkv, w_out, w_up, w_down)
    grad_second, gain_second, shift_second = second_pullback(cotangent)
    grad_ffn_low = grad_second.astype(jnp.bfloat16)
    grad_down = jnp.einsum("tf,td->fd", act_low, grad_ffn_low, preferred_element_type=jnp.float32)
    grad_act = jnp.einsum("td,fd->tf", grad_ffn_low, back_down, preferred_element_type=jnp.float32)
    (grad_pre,) = gelu_pullback(grad_act)
    grad_pre_low = grad_pre.astype(jnp.bfloat16)
    grad_up = jnp.einsum("td,tf->df", normed_low, grad_pre_low, preferred_element_type=jnp.float32)
    up_part = jnp.einsum("tf,df->td", grad_pre_low, back_up, preferred_element_type=jnp.float32)
    grad_normed = across_heads(up_part) + grad_second
    grad_first, gain_first, shift_first = first_pullback(grad_normed)
    grad_attn_low = grad_first.astype(jnp.bfloat16)
    grad_out = jnp.einsum("th,td->hd", heads_low, grad_attn_low, preferred_element_type=jnp.float32)
    grad_heads = (
        jnp.einsum("td,hd->th", grad_attn_low, back_out, preferred_element_type=jnp.float32)
        .astype(jnp.bfloat16)
        .reshape(seq_count, half_len, head_cols)
    )
    grad_query, grad_key_all, grad_value_all = lax.map(
        attend_backward,
        (query_low, key_all, value_all, labels_query, segments, grad_heads, log_total),
    )
    grad_key, grad_value = (
        lax.psum_scatter(
            grad_key_all.astype(jnp.bfloat16), "ctx", scatter_dimension=1, tiled=True
        ).astype(jnp.float32),
        lax.psum_scatter(
            grad_value_all.astype(jnp.bfloat16), "ctx", scatter_dimension=1, tiled=True
        ).astype(jnp.float32),
    )
    grad_query = grad_query.reshape(row_count, head_cols)
    grad_key = grad_key.reshape(row_count, head_cols)
    grad_value = grad_value.reshape(row_count, head_cols)
    grad_prod_low = jnp.stack([grad_query, grad_key, grad_value], axis=1).astype(jnp.bfloat16)
    grad_qkv = jnp.einsum(
        "td,tcf->dcf", stream_low, grad_prod_low, preferred_element_type=jnp.float32
    )
    qkv_part = jnp.einsum(
        "tcf,dcf->td", grad_prod_low, back_qkv, preferred_element_type=jnp.float32
    )
    qv_term = jnp.stack([jnp.sum(grad_query, axis=0), jnp.sum(grad_value, axis=0)])
    up_term = jnp.sum(grad_pre, axis=0)
    gain_term = jnp.stack([gain_first, gain_second])
    shift_term = jnp.stack([shift_first, shift_second])
    bias_term = jnp.stack([jnp.sum(grad_first, axis=0), jnp.sum(grad_second, axis=0)])
    input_grad = across_heads(qkv_part) + grad_first
    qv_sum, up_sum, gain_sum, shift_sum, bias_sum = lax.psum(
        (qv_term, up_term, gain_term, shift_term, bias_term), ("shard", "ctx")
    )
    shares = (
        lax.psum_scatter(
            grad_qkv.astype(jnp.bfloat16), "shard", scatter_dimension=0, tiled=True
        ).astype(jnp.float32),
        lax.psum_scatter(
            grad_out.astype(jnp.bfloat16), "shard", scatter_dimension=1, tiled=True
        ).astype(jnp.float32),
        lax.psum_scatter(
            grad_up.astype(jnp.bfloat16), "shard", scatter_dimension=0, tiled=True
        ).astype(jnp.float32),
        lax.psum_scatter(
            grad_down.astype(jnp.bfloat16), "shard", scatter_dimension=1, tiled=True
        ).astype(jnp.float32),
    )
    qkv_share, out_share, up_share, down_share = (
        lax.psum(shares[0].astype(jnp.bfloat16), "ctx").astype(jnp.float32),
        lax.psum(shares[1].astype(jnp.bfloat16), "ctx").astype(jnp.float32),
        lax.psum(shares[2].astype(jnp.bfloat16), "ctx").astype(jnp.float32),
        lax.psum(shares[3].astype(jnp.bfloat16), "ctx").astype(jnp.float32),
    )
    return (
        layer_rows.reshape(seq_count, half_len, model_width),
        input_grad.reshape(seq_count, half_len, model_width),
        qkv_share,
        out_share,
        up_share,
        down_share,
        qv_sum,
        up_sum,
        gain_sum,
        shift_sum,
        bias_sum,
    )


def solution(mesh):
    placed = (
        P("shard", "ctx", None),
        P("shard", None),
        P("shard", None),
        P("shard", None, "tp"),
        P("tp", "shard"),
        P("shard", "tp"),
        P("tp", "shard"),
        P(None, "tp"),
        P("tp"),
        P(),
        P(),
        P(),
        P("shard", "ctx", None),
    )
    return jax.shard_map(
        shards,
        mesh=mesh,
        in_specs=placed,
        out_specs=(
            P("shard", "ctx", None),
            P("shard", "ctx", None),
            P("shard", None, "tp"),
            P("tp", "shard"),
            P("shard", "tp"),
            P("tp", "shard"),
            P(None, "tp"),
            P("tp"),
            P(),
            P(),
            P(),
        ),
        check_vma=False,
    )
```

profile of v0, /device:TPU:0, one launch (start us, length us, event | category | flops | bytes accessed | tf_op | source)
XLA Modules:
  0.0 712.3 jit_solution(5007047133472476936)
XLA Ops:
  8.9 25.9 %all_gather.22 = bf16[768,3,192]{2,0,1:T(8,128)(2,1)S(1)} all-gather(bf16[192,3,192]{2,0,1:T(8,128)(2,1)} %param.20), channel_id=1, replica_groups=mesh['shard'=4,'ctx'=2,'tp'=4] {'shard'}, dimensions={0}, use_global_device_ids=true | all-gather | bytes 1105920 | tf_op jit(solution)/shard_map/all_gather | solution.py:21
  36.1 2.0 convert_add_fusion
  40.2 14.4 %all_gather.25 = bf16[192,768]{0,1:T(8,128)(2,1)S(1)} all-gather(bf16[192,192]{0,1:T(8,128)(2,1)S(1)} %copy.47), channel_id=1, replica_groups=mesh['shard'=4,'ctx'=2,'tp'=4] {'shard'}, dimensions={1}, use_global_device_ids=true | all-gather | bytes 368640 | tf_op jit(solution)/shard_map/all_gather | solution.py:22
  56.5 2.4 all_gather.24
  59.8 2.4 all_gather.23
  63.5 14.4 %while.28 = (s32[]{:T(128)}, bf16[2,512,192]{1,2,0:T(8,128)(2,1)}, f32[2,3,512]{2,1,0:T(4,128)}, bf16[2,1024,192]{1,2,0:T(8,128)(2,1)S(1)}, s32[2,512]{1,0:T(2,1...) while((s32[]{:T(128)}, bf16[2,512,192]{1,2,0:T(8,128)(2,1)}, ...), condition=%wide.region_3.4_spmd.clone, body=%wide.region_0.3_spmd.sunk.clone | while | flops 422050304 | bytes 27828452 | solution.py:140
  67.1 2.1 fusion.121
  72.5 1.7 fusion.120
  74.3 2.1 fusion.121
  79.2 2.3 fusion.50
  85.1 84.7 %all-reduce.8.cloned.1.call-done = f32[1024,768]{1,0:T(8,128)} async-done(((f32[1024,768]{1,0:T(8,128)}), f32[1024,768]{1,0:T(8,128)}) %all-reduce.8.cloned.1.call-update) | async-done | bytes 3145744 | tf_op jit(solution)/shard_map/psum | solution.py:29
  169.7 3.3 fusion.42
  174.7 11.4 %multiply_convert_fusion.1 = (bf16[1024,768]{1,0:T(8,128)(2,1)}, f32[1024,768]{1,0:T(8,128)}, f32[1024,768]{1,0:T(8,128)}) fusion(f32[768]{0:T(1024)} %param.25, bf16[768,768]{1,0:T(8,128)(2,1)} %all-gather.3.cloned.1.call-done, f32[1024,768]{1,0:T(8,128)S(1)} %get-tuple-element.219, f32[768]{0:T(1024)} %get-tuple-element.159, f32[768]{0:T(1024)} %get-tuple-element.157, ...), kind=kOutput, calls=%fused_computation.56 | convolution fusion | flops 1263796224 | bytes 12207104 | tf_op jit(solution)/shard_map/dot_general | solution.py:150
  186.1 4.8 fusion.51
  191.0 87.1 %all-reduce.10.cloned.1.call-done = f32[1024,768]{1,0:T(8,128)} async-done(((f32[1024,768]{1,0:T(8,128)}), f32[1024,768]{1,0:T(8,128)}) %all-reduce.10.cloned.1.call-update) | async-done | bytes 3145744 | tf_op jit(solution)/shard_map/psum | solution.py:29
  278.1 2.9 fusion.40
  282.4 1.8 fusion.15
  284.2 2.8 fusion.39
  287.4 2.2 copy-done.55
  289.7 3.2 fusion.46
  294.0 3.1 fusion.32
  297.4 86.9 %all-reduce.12.cloned.1.call-done = f32[1024,768]{1,0:T(8,128)} async-done(((f32[1024,768]{1,0:T(8,128)}), f32[1024,768]{1,0:T(8,128)}) %all-reduce.12.cloned.1.call-update) | async-done | bytes 3145744 | tf_op jit(solution)/shard_map/psum | solution.py:29
  384.3 5.0 multiply_reduce_fusion.1
  394.1 30.5 %while.29 = (s32[]{:T(128)}, f32[2,512,192]{1,2,0:T(8,128)}, bf16[2,1024,192]{1,2,0:T(8,128)(2,1)}, bf16[2,1024,192]{1,2,0:T(8,128)(2,1)}, bf16[2,1024,192]{1,2,...) while((s32[]{:T(128)}, f32[2,512,192]{1,2,0:T(8,128)}, ...), condition=%wide.region_17.18_spmd.clone, body=%wide.region_15.17_spmd.sunk.clone | while | flops 1031240192 | bytes 76083512 | solution.py:176
  399.2 1.9 fusion.133
  401.1 2.5 multiply_reduce_fusion.7
  403.6 1.8 multiply_convert_fusion.4
  414.5 1.9 fusion.133
  416.4 2.5 multiply_reduce_fusion.7
  418.9 1.8 multiply_convert_fusion.4
  425.4 2.6 convolution_convert_fusion.3
  429.2 5.2 convolution_convert_fusion
  434.5 4.2 convolution_convert_fusion.1
  438.8 2.1 bitcast_convert_fusion
  448.1 3.8 fusion.24
  452.0 17.1 %reduce-scatter.19.cloned.1.call-done = bf16[192,192]{1,0:T(8,128)(2,1)} async-done(((bf16[768,192]{1,0:T(8,128)(2,1)}), bf16[192,192]{1,0:T(8,128)(2,1)}) %reduce-scatter.19.cloned.1.call-update) | async-done | bytes 73744
  470.7 28.3 %reduce-scatter.17.cloned.1.call-done = bf16[768,192]{0,1:T(8,128)(2,1)} async-done(((bf16[768,768]{0,1:T(8,128)(2,1)}), bf16[768,192]{0,1:T(8,128)(2,1)}) %reduce-scatter.17.cloned.1.call-update) | async-done | bytes 294928 | tf_op jit(solution)/shard_map/reduce_scatter | solution.py:217
  499.0 30.1 %reduce-scatter.15.cloned.1.call-done = bf16[192,768]{1,0:T(8,128)(2,1)} async-done(((bf16[768,768]{1,0:T(8,128)(2,1)}), bf16[192,768]{1,0:T(8,128)(2,1)}) %reduce-scatter.15.cloned.1.call-update) | async-done | bytes 294928 | tf_op jit(solution)/shard_map/reduce_scatter | solution.py:214
  529.1 30.6 %reduce-scatter.13.cloned.1.call-done = bf16[192,3,192]{2,0,1:T(8,128)(2,1)} async-done(((bf16[768,3,192]{2,0,1:T(8,128)(2,1)}), bf16[192,3,192]{2,0,1:T(8,128)(2,1)}) %reduce-scatter.13.cloned.1.call-update) | async-done | bytes 221200 | tf_op jit(solution)/shard_map/reduce_scatter | solution.py:208
  559.8 4.4 convolution_bitcast_fusion
  564.3 1.8 convert_reduce_fusion
  568.3 12.1 %all-reduce.16.cloned.1.call-done = (bf16[192,3,192]{2,0,1:T(8,128)(2,1)}, bf16[192,192]{1,0:T(8,128)(2,1)}, bf16[192,768]{1,0:T(8,128)(2,1)}, bf16[768,192]{0,1:T(8,128)(2,1)}) async-done(((bf16[192,3,192]{2,0,1:T(8,128)(2,1)}, bf16[192,192]{1,0:T(8,128)(2,1)}, bf16[192,768]{1,0:T(8,128)(2,1)}, bf16[768,192]{0,1:T(8,128)(2,1)}), (bf16[192,3,192]{2,0,1:T(8,128)(2,1)}, bf16[192,192]{1,0:T(8,128)(2,1)}, ...) | async-done | bytes 884752 | tf_op jit(solution)/shard_map/psum | solution.py:222
  582.0 1.8 convert_element_type.122
  583.8 1.8 convert_element_type.126
  585.6 1.8 convert_element_type.128
  587.5 84.6 %all-reduce.14.cloned.1.call-done = f32[1024,768]{1,0:T(8,128)} async-done(((f32[1024,768]{1,0:T(8,128)}), f32[1024,768]{1,0:T(8,128)}) %all-reduce.14.cloned.1.call-update) | async-done | bytes 3145744 | tf_op jit(solution)/shard_map/psum | solution.py:29
  672.1 4.0 add_reduce_fusion
  676.1 28.9 %all-reduce = (f32[2,192]{1,0:T(2,128)}, f32[768]{0:T(1024)}, f32[2,768]{1,0:T(2,128)}, f32[2,768]{1,0:T(2,128)}, f32[2,768]{1,0:T(2,128)}) all-reduce(f32[2,192]{1,0:T(2,128)S(1)} %pad_maximum_fusion.3, f32[768]{0:T(1024)S(1)} %copy-done.48, ...), channel_id=1, replica_groups=mesh['shard'=4,'ctx'=2,'tp'=4] {'shard','ctx'}, use_global_device_ids=true, to_apply=%region_31.32 | all-reduce | flops 5760 | bytes 46080 | tf_op jit(solution)/shard_map/psum | solution.py:204
  (262 shorter events, 63.6 us)
Async XLA Ops:
  8.0 28.1 %copy-start.44 = (f32[2,768]{1,0:T(2,128)S(1)}, f32[2,768]{1,0:T(2,128)}, u32[]{:S(2)}) copy-start(f32[2,768]{1,0:T(2,128)} %param.18) | copy-start | bytes 18436
  8.0 28.1 %copy-start.14 = (bf16[2,512,768]{2,1,0:T(8,128)(2,1)S(1)}, bf16[2,512,768]{2,1,0:T(8,128)(2,1)}, u32[]{:S(2)}) copy-start(bf16[2,512,768]{2,1,0:T(8,128)(2,1)} %param.17) | copy-start | bytes 4718596
  8.0 161.7 %all-reduce.8.cloned.1.call-start = ((), (), s32[]{:S(2)}) async-start(), calls=%async_computation.6 | async-start | bytes 6291456 | tf_op jit(solution)/shard_map/psum | solution.py:29
  34.7 3.4 copy-start.6
  54.6 24.5 %copy-start.9 = (bf16[192,768]{0,1:T(8,128)(2,1)}, bf16[192,768]{0,1:T(8,128)(2,1)S(1)}, u32[]{:S(2)}) copy-start(bf16[192,768]{0,1:T(8,128)(2,1)S(1)} %all_gather.25) | copy-start | bytes 884740
  56.5 5.7 copy-start.23
  77.8 3.7 copy-start.2
  77.8 3.7 copy-start.3
  79.1 4.1 copy-start.45
  79.2 4.7 copy-start.46
  79.2 5.3 copy-start.47
  81.5 93.2 %all-gather.3.cloned.1.call-start = ((), (), s32[]{:S(2)}) async-start(), calls=%async_computation.7 | async-start | bytes 1474560 | tf_op jit(solution)/shard_map/all_gather | solution.py:23
  82.1 104.0 %all-gather.5.cloned.1.call-start = ((), (), s32[]{:S(2)}) async-start(), calls=%async_computation.8 | async-start | bytes 1474560 | tf_op jit(solution)/shard_map/all_gather | solution.py:24
  82.7 195.4 %all-reduce.10.cloned.1.call-start = ((), (), s32[]{:S(2)}) async-start(), calls=%async_computation.9 | async-start | bytes 6291456 | tf_op jit(solution)/shard_map/psum | solution.py:29
  191.0 193.3 %all-reduce.12.cloned.1.call-start = ((), (), s32[]{:S(2)}) async-start(), calls=%async_computation.10 | async-start | bytes 6291456 | tf_op jit(solution)/shard_map/psum | solution.py:29
  281.5 2.7 copy-start.38
  284.2 2.9 copy-start.51
  284.2 2.9 copy-start.52
  284.2 3.2 copy-start.54
  284.2 5.5 copy-start.55
  287.0 5.8 copy-start.5
  287.0 5.8 copy-start.42
  289.7 4.4 copy-start.50
  297.2 145.9 %reduce-scatter.9.cloned.1.call-start = ((), (), s32[]{:S(2)}) async-start(), calls=%async_computation.11 | async-start | bytes 1179648 | tf_op jit(solution)/shard_map/reduce_scatter | solution.py:181
  384.3 5.0 copy-start.34
  384.3 5.0 copy-start.27
  384.3 5.0 copy-start.31
  389.3 3.1 copy-start.10
  390.8 3.2 copy-start.29
  424.6 4.6 copy-start.43
  424.6 20.2 %reduce-scatter.11.cloned.1.call-start = ((), (), s32[]{:S(2)}) async-start(), calls=%async_computation.12 | async-start | bytes 1179648 | tf_op jit(solution)/shard_map/reduce_scatter | solution.py:184
  425.3 43.8 %reduce-scatter.19.cloned.1.call-start = ((), (), s32[]{:S(2)}) async-start(), calls=%async_computation.17 | async-start | bytes 491520
  428.9 5.6 copy-start.28
  428.9 5.6 copy-start.32
  428.9 5.6 copy-start.37
  428.9 70.1 %reduce-scatter.17.cloned.1.call-start = ((), (), s32[]{:S(2)}) async-start(), calls=%async_computation.16 | async-start | bytes 1474560 | tf_op jit(solution)/shard_map/reduce_scatter | solution.py:217
  434.4 94.7 %reduce-scatter.15.cloned.1.call-start = ((), (), s32[]{:S(2)}) async-start(), calls=%async_computation.15 | async-start | bytes 1474560 | tf_op jit(solution)/shard_map/reduce_scatter | solution.py:214
  438.8 120.9 %reduce-scatter.13.cloned.1.call-start = ((), (), s32[]{:S(2)}) async-start(), calls=%async_computation.14 | async-start | bytes 1474560 | tf_op jit(solution)/shard_map/reduce_scatter | solution.py:208
  448.1 111.7 %copy-start.7 = (bf16[768,3,192]{2,0,1:T(8,128)(2,1)S(1)}, bf16[768,3,192]{2,0,1:T(8,128)(2,1)}, u32[]{:S(2)}) copy-start(bf16[768,3,192]{2,0,1:T(8,128)(2,1)} %copy-done.6) | copy-start | bytes 2654212
  451.9 128.5 %all-reduce.16.cloned.1.call-start = ((), (), s32[]{:S(2)}) async-start(), calls=%async_computation.18 | async-start | bytes 1966080 | tf_op jit(solution)/shard_map/psum | solution.py:222
  559.8 112.3 %all-reduce.14.cloned.1.call-start = ((), (), s32[]{:S(2)}) async-start(), calls=%async_computation.13 | async-start | bytes 6291456 | tf_op jit(solution)/shard_map/psum | solution.py:29
  564.2 2.6 copy-start.40
  564.2 2.6 copy-start.39
  564.2 3.3 copy-start.11
  564.3 107.8 %copy-start.1 = (f32[1024,768]{1,0:T(8,128)S(1)}, f32[1024,768]{1,0:T(8,128)}, u32[]{:S(2)}) copy-start(f32[1024,768]{1,0:T(8,128)} %copy-done) | copy-start | bytes 9437188
  564.3 107.8 %copy-start.30 = (f32[1024]{0:T(1024)S(1)}, f32[1024]{0:T(1024)}, u32[]{:S(2)}) copy-start(f32[1024]{0:T(1024)} %copy-done.29) | copy-start | bytes 12292
  587.5 88.6 %copy-start.36 = (f32[2,768]{1,0:T(2,128)S(1)}, f32[2,768]{1,0:T(2,128)}, u32[]{:S(2)}) copy-start(f32[2,768]{1,0:T(2,128)} %get-tuple-element.244) | copy-start | bytes 18436
  587.5 88.6 %copy-start.48 = (f32[768]{0:T(1024)S(1)}, f32[768]{0:T(1024)}, u32[]{:S(2)}) copy-start(f32[768]{0:T(1024)} %get-tuple-element.241) | copy-start | bytes 9220
  (31 other events, 43.6 us)
Sparse Core Ops, SparseCore 0:
  81.6 88.0 all-reduce.7
  191.1 86.9 all-reduce.9
  297.3 86.9 all-reduce.11
Sparse Core Ops, SparseCore 1:
  83.6 31.2 all-gather.2
  116.2 29.3 all-gather.4
  424.7 8.1 reduce-scatter.8
  435.1 9.2 reduce-scatter.10
  447.2 21.8 reduce-scatter.18
  471.4 27.5 reduce-scatter.16
  501.2 27.8 reduce-scatter.14
  531.9 27.8 reduce-scatter.12
  562.7 17.6 all-reduce.15
  584.1 87.9 all-reduce.13
where the time goes:
time: 720 us; the launch traced here: 712 us
  waiting for transfers between devices  463 us (64%)
  blocking collectives  73.9 us (10%)
  matrix products  68.3 us (9%)
  other arithmetic  48.8 us (7%)
  local copies, waits for them, and re-layouts  39.9 us (6%)
  between operations  16.2 us (2%)
    psum x4, waiting for transfers between devices, across_heads(): return lax.psum(term_rows, 'tp')  343 us
    reduce_scatter x1, waiting for transfers between devices, shards(): lax.psum_scatter(grad_qkv.astype(jnp.bfloat16), 'shard', scatter_dimensio...  30.6 us
    reduce_scatter x1, waiting for transfers between devices, shards(): lax.psum_scatter(grad_up.astype(jnp.bfloat16), 'shard', scatter_dimension...  30.1 us
    psum x1, blocking collectives, shards(): lax.psum((qv_term, up_term, gain_term, shift_term, bias_term), ('shard',...  28.9 us
    reduce_scatter x1, waiting for transfers between devices, shards(): lax.psum_scatter(grad_down.astype(jnp.bfloat16), 'shard', scatter_dimensi...  28.3 us
    all_gather x1, blocking collectives, fetch_weights(): lax.all_gather(w_qkv, 'shard', axis=0, tiled=True)  25.9 us
    unnamed x14, waiting for transfers between devices  19 us
    all_gather x1, blocking collectives, fetch_weights(): lax.all_gather(w_out, 'shard', axis=1, tiled=True)  14.4 us
  transfers between devices with their start and end apart: 13, of which 9 were waited for; matrix products, arithmetic and copies ran while one was open for 9% of the time, Pallas kernels for 0%

commit v1 on v0

--- a/solution.py
+++ b/solution.py
@@ -1,9 +1,18 @@
+import functools
 import jax
 import jax.numpy as jnp
 from jax import lax
 from jax.sharding import PartitionSpec as P
 
 HD = 64
+
+
+def show_hubs_by_axis(local, ax_name):
+    right_arr = lax.all_gather(local, ax_name).sum(axis=0)
+    return right_arr
+
+
+raise_streams = functools.partial(show_hubs_by_axis, ax_name="tp")
 
 
 def layer_norm(residual, gain_vec, shift_vec):
@@ -26,7 +35,7 @@
 
 
 def across_heads(term_rows):
-    return lax.psum(term_rows, "tp")
+    return raise_streams(term_rows)
 
 
 def masked_scores(query_blk, key_blk, labels_query, labels_key):

time: 720 us -> 933 us (1.30)
  waiting for transfers between devices: 463 us -> 642 us
  other arithmetic: 48.8 us -> 82.2 us
    all_gather x0 -> x4, waiting for transfers between devices: none -> 483 us  [show_hubs_by_axis(): right_arr = lax.all_gather(local, ax_name).sum(axis=0)]
    psum x4 -> x0, waiting for transfers between devices: 343 us -> none  [across_heads(): return lax.psum(term_rows, 'tp')]
    reduce_sum x0 -> x5, other arithmetic: none -> 38.1 us  [the longest x4 30.1 us: show_hubs_by_axis(): right_arr = lax.all_gather(local, ax_name).sum(axis=0)]
    all_gather x1, waiting for transfers between devices: 0.01 us -> 19.6 us  [fetch_weights(): lax.all_gather(w_down, 'shard', axis=1, tiled=True)]
    all_gather x1, waiting for transfers between devices: 0.01 us -> 15.6 us  [fetch_weights(): lax.all_gather(w_up, 'shard', axis=0, tiled=True)]
  transfers between devices with their start and end apart: 13 -> 13, of which waited for: 9 -> 11; matrix products, arithmetic and copies ran while one was open for 9% -> 7% of each run, Pallas kernels for 0% -> 0%
where the time goes in v1:
time: 933 us; the launch traced here: 925 us
  waiting for transfers between devices  642 us (69%)
  other arithmetic  82.2 us (9%)
  blocking collectives  74.1 us (8%)
  matrix products  68.5 us (7%)
  local copies, waits for them, and re-layouts  41.2 us (4%)
  between operations  14.9 us (2%)
    all_gather x4, waiting for transfers between devices, show_hubs_by_axis(): right_arr = lax.all_gather(local, ax_name).sum(axis=0)  483 us
    reduce_scatter x1, waiting for transfers between devices, shards(): lax.psum_scatter(grad_qkv.astype(jnp.bfloat16), 'shard', scatter_dimensio...  30.9 us
    reduce_scatter x1, waiting for transfers between devices, shards(): lax.psum_scatter(grad_up.astype(jnp.bfloat16), 'shard', scatter_dimension...  30.1 us
    reduce_sum x4, other arithmetic, show_hubs_by_axis(): right_arr = lax.all_gather(local, ax_name).sum(axis=0)  30.1 us
    psum x1, blocking collectives, shards(): lax.psum((qv_term, up_term, gain_term, shift_term, bias_term), ('shard',...  29 us
    reduce_scatter x1, waiting for transfers between devices, shards(): lax.psum_scatter(grad_down.astype(jnp.bfloat16), 'shard', scatter_dimensi...  28.3 us
    all_gather x1, blocking collectives, fetch_weights(): lax.all_gather(w_qkv, 'shard', axis=0, tiled=True)  26 us
    unnamed x14, waiting for transfers between devices  19.6 us
  transfers between devices with their start and end apart: 13, of which 11 were waited for; matrix products, arithmetic and copies ran while one was open for 7% of the time, Pallas kernels for 0%

profile of v1, /device:TPU:0, one launch (start us, length us, event | category | flops | bytes accessed | tf_op | source)
XLA Modules:
  0.0 925.0 jit_solution(1125531877590279072)
XLA Ops:
  7.3 26.0 %all_gather.46 = bf16[768,3,192]{2,0,1:T(8,128)(2,1)S(1)} all-gather(bf16[192,3,192]{2,0,1:T(8,128)(2,1)} %param.20), channel_id=1, replica_groups=mesh['shard'=4,'ctx'=2,'tp'=4] {'shard'}, dimensions={0}, use_global_device_ids=true | all-gather | bytes 1105920 | tf_op jit(solution)/shard_map/all_gather | solution.py:30
  34.7 2.0 convert_add_fusion
  38.8 14.4 %all_gather.49 = bf16[192,768]{0,1:T(8,128)(2,1)S(1)} all-gather(bf16[192,192]{0,1:T(8,128)(2,1)S(1)} %copy.47), channel_id=1, replica_groups=mesh['shard'=4,'ctx'=2,'tp'=4] {'shard'}, dimensions={1}, use_global_device_ids=true | all-gather | bytes 368640 | tf_op jit(solution)/shard_map/all_gather | solution.py:31
  55.1 2.4 all_gather.48
  60.4 2.4 all_gather.47
  64.1 12.8 %while.28 = (s32[]{:T(128)}, bf16[2,512,192]{1,2,0:T(8,128)(2,1)S(1)}, f32[2,3,512]{2,1,0:T(4,128)}, bf16[2,1024,192]{1,2,0:T(8,128)(2,1)S(1)}, s32[2,512]{1,0:T...) while((s32[]{:T(128)}, ...), condition=%wide.region_3.4_spmd.clone, body=%wide.region_0.3_spmd.sunk.clone | while | flops 422050304 | bytes 24580212 | solution.py:149
  67.7 2.1 fusion.144
  74.2 2.1 fusion.144
  77.1 2.3 fusion.73
  83.0 120.1 %all-gather.15.cloned.1.call-done = f32[4096,768]{1,0:T(8,128)} async-done(((f32[1024,768]{1,0:T(8,128)}), f32[4096,768]{1,0:T(8,128)}) %all-gather.15.cloned.1.call-update) | async-done | bytes 12582928 | tf_op jit(solution)/shard_map/all_gather | solution.py:11
  203.1 7.5 reduce_sum.251
  210.5 3.3 fusion.66
  217.3 2.0 add_subtract_fusion
  219.3 15.6 %all-gather.11.cloned.1.call-done = bf16[768,768]{1,0:T(8,128)(2,1)} async-done(((bf16[192,768]{1,0:T(8,128)(2,1)}), bf16[768,768]{1,0:T(8,128)(2,1)}) %all-gather.11.cloned.1.call-update) | async-done | bytes 1179664 | tf_op jit(solution)/shard_map/all_gather | solution.py:32
  234.9 11.6 %multiply_convert_fusion.1 = (bf16[1024,768]{1,0:T(8,128)(2,1)}, f32[1024,768]{1,0:T(8,128)}, f32[1024,768]{1,0:T(8,128)}) fusion(f32[768]{0:T(1024)} %param.25, bf16[768,768]{1,0:T(8,128)(2,1)} %all-gather.11.cloned.1.call-done, f32[1024,768]{1,0:T(8,128)} %add_subtract_fusion, f32[768]{0:T(1024)} %get-tuple-element.162, f32[768]{0:T(1024)S(1)} %get-tuple-element.160, ...), kind=kOutput, calls=%fused_computation.56 | convolution fusion | flops 1263009792 | bytes 12203008 | tf_op jit(solution)/shard_map/dot_general | solution.py:159
  246.5 19.6 %all-gather.13.cloned.1.call-done = bf16[768,768]{0,1:T(8,128)(2,1)} async-done(((bf16[768,192]{0,1:T(8,128)(2,1)}), bf16[768,768]{0,1:T(8,128)(2,1)}) %all-gather.13.cloned.1.call-update) | async-done | bytes 1179664 | tf_op jit(solution)/shard_map/all_gather | solution.py:33
  266.0 4.8 fusion.74
  271.1 121.5 %all-gather.17.cloned.1.call-done = f32[4096,768]{1,0:T(8,128)} async-done(((f32[1024,768]{1,0:T(8,128)}), f32[4096,768]{1,0:T(8,128)}) %all-gather.17.cloned.1.call-update) | async-done | bytes 12582928 | tf_op jit(solution)/shard_map/all_gather | solution.py:11
  392.6 7.5 reduce_sum.255
  400.1 3.0 fusion.64
  409.4 2.1 copy-done.67
  411.5 2.9 fusion.71
  415.6 3.1 fusion.43
  419.2 122.1 %all-gather.19.cloned.1.call-done = f32[4096,768]{1,0:T(8,128)} async-done(((f32[1024,768]{1,0:T(8,128)}), f32[4096,768]{1,0:T(8,128)}) %all-gather.19.cloned.1.call-update) | async-done | bytes 12582928 | tf_op jit(solution)/shard_map/all_gather | solution.py:11
  541.2 7.5 reduce_sum.262
  548.7 8.1 add_reduce_fusion
  556.9 2.3 fusion.63
  564.2 30.7 %while.29 = (s32[]{:T(128)}, f32[2,512,192]{1,2,0:T(8,128)}, bf16[2,1024,192]{1,2,0:T(8,128)(2,1)}, bf16[2,1024,192]{1,2,0:T(8,128)(2,1)}, bf16[2,1024,192]{1,2,...) while((s32[]{:T(128)}, f32[2,512,192]{1,2,0:T(8,128)}, ...), condition=%wide.region_17.18_spmd.clone, body=%wide.region_15.17_spmd.sunk.clone | while | flops 1031240192 | bytes 76083512 | solution.py:185
  569.6 1.9 fusion.156
  571.4 2.5 multiply_reduce_fusion.9
  584.8 1.9 fusion.156
  586.7 2.5 multiply_reduce_fusion.9
  598.5 4.8 convolution_convert_fusion
  603.5 5.1 convolution_convert_fusion.1
  618.3 3.8 fusion.29
  622.2 17.4 %reduce-scatter.19.cloned.1.call-done = bf16[192,192]{1,0:T(8,128)(2,1)} async-done(((bf16[768,192]{1,0:T(8,128)(2,1)}), bf16[192,192]{1,0:T(8,128)(2,1)}) %reduce-scatter.19.cloned.1.call-update) | async-done | bytes 73744
  641.2 28.3 %reduce-scatter.17.cloned.1.call-done = bf16[768,192]{0,1:T(8,128)(2,1)} async-done(((bf16[768,768]{0,1:T(8,128)(2,1)}), bf16[768,192]{0,1:T(8,128)(2,1)}) %reduce-scatter.17.cloned.1.call-update) | async-done | bytes 294928 | tf_op jit(solution)/shard_map/reduce_scatter | solution.py:226
  669.5 30.1 %reduce-scatter.15.cloned.1.call-done = bf16[192,768]{1,0:T(8,128)(2,1)} async-done(((bf16[768,768]{1,0:T(8,128)(2,1)}), bf16[192,768]{1,0:T(8,128)(2,1)}) %reduce-scatter.15.cloned.1.call-update) | async-done | bytes 294928 | tf_op jit(solution)/shard_map/reduce_scatter | solution.py:223
  699.6 30.9 %reduce-scatter.13.cloned.1.call-done = bf16[192,3,192]{2,0,1:T(8,128)(2,1)} async-done(((bf16[768,3,192]{2,0,1:T(8,128)(2,1)}), bf16[192,3,192]{2,0,1:T(8,128)(2,1)}) %reduce-scatter.13.cloned.1.call-update) | async-done | bytes 221200 | tf_op jit(solution)/shard_map/reduce_scatter | solution.py:217
  730.6 4.4 convolution_bitcast_fusion
  736.1 15.5 %all-reduce.4.cloned.1.call-done = (bf16[192,3,192]{2,0,1:T(8,128)(2,1)}, bf16[192,192]{1,0:T(8,128)(2,1)}, bf16[192,768]{1,0:T(8,128)(2,1)}, bf16[768,192]{0,1:T(8,128)(2,1)}) async-done(((bf16[192,3,192]{2,0,1:T(8,128)(2,1)}, bf16[192,192]{1,0:T(8,128)(2,1)}, bf16[192,768]{1,0:T(8,128)(2,1)}, bf16[768,192]{0,1:T(8,128)(2,1)}), (bf16[192,3,192]{2,0,1:T(8,128)(2,1)}, bf16[192,192]{1,0:T(8,128)(2,1)}, ...) | async-done | bytes 884752 | tf_op jit(solution)/shard_map/psum | solution.py:231
  753.2 1.8 convert_element_type.126
  755.0 1.8 convert_element_type.131
  756.8 1.8 convert_element_type.133
  758.6 119.0 %all-gather.21.cloned.1.call-done = f32[4096,768]{1,0:T(8,128)} async-done(((f32[1024,768]{1,0:T(8,128)}), f32[4096,768]{1,0:T(8,128)}) %all-gather.21.cloned.1.call-update) | async-done | bytes 12582928 | tf_op jit(solution)/shard_map/all_gather | solution.py:11
  877.7 7.6 reduce_sum.267
  885.3 4.0 add_reduce_fusion.1
  889.3 29.0 %all-reduce = (f32[2,192]{1,0:T(2,128)}, f32[768]{0:T(1024)}, f32[2,768]{1,0:T(2,128)}, f32[2,768]{1,0:T(2,128)}, f32[2,768]{1,0:T(2,128)}) all-reduce(f32[2,192]{1,0:T(2,128)S(1)} %pad_maximum_fusion.3, f32[768]{0:T(1024)S(1)} %copy-done.60, ...), channel_id=1, replica_groups=mesh['shard'=4,'ctx'=2,'tp'=4] {'shard','ctx'}, use_global_device_ids=true, to_apply=%region_31.32 | all-reduce | flops 5760 | bytes 46080 | tf_op jit(solution)/shard_map/psum | solution.py:213
  (292 shorter events, 77.5 us)
Async XLA Ops:
  7.2 27.5 %copy-start.51 = (f32[2,768]{1,0:T(2,128)S(1)}, f32[2,768]{1,0:T(2,128)}, u32[]{:S(2)}) copy-start(f32[2,768]{1,0:T(2,128)} %param.18) | copy-start | bytes 18436
  7.2 27.5 %copy-start.15 = (bf16[2,512,768]{2,1,0:T(8,128)(2,1)S(1)}, bf16[2,512,768]{2,1,0:T(8,128)(2,1)}, u32[]{:S(2)}) copy-start(bf16[2,512,768]{2,1,0:T(8,128)(2,1)} %param.17) | copy-start | bytes 4718596
  7.2 195.9 %all-gather.15.cloned.1.call-start = ((), (), s32[]{:S(2)}) async-start(), calls=%async_computation.13 | async-start | bytes 15728640 | tf_op jit(solution)/shard_map/all_gather | solution.py:11
  33.3 3.4 copy-start.16
  53.3 23.8 %copy-start.18 = (bf16[192,768]{0,1:T(8,128)(2,1)}, bf16[192,768]{0,1:T(8,128)(2,1)S(1)}, u32[]{:S(2)}) copy-start(bf16[192,768]{0,1:T(8,128)(2,1)S(1)} %all_gather.49) | copy-start | bytes 884740
  55.1 7.7 copy-start.30
  77.0 4.1 copy-start.57
  77.0 4.7 copy-start.58
  77.1 5.3 copy-start.59
  79.4 155.5 %all-gather.11.cloned.1.call-start = ((), (), s32[]{:S(2)}) async-start(), calls=%async_computation.6 | async-start | bytes 1474560 | tf_op jit(solution)/shard_map/all_gather | solution.py:32
  80.2 185.9 %all-gather.13.cloned.1.call-start = ((), (), s32[]{:S(2)}) async-start(), calls=%async_computation.7 | async-start | bytes 1474560 | tf_op jit(solution)/shard_map/all_gather | solution.py:33
  80.9 311.7 %all-gather.17.cloned.1.call-start = ((), (), s32[]{:S(2)}) async-start(), calls=%async_computation.14 | async-start | bytes 15728640 | tf_op jit(solution)/shard_map/all_gather | solution.py:11
  210.5 6.8 copy-start.9
  213.8 3.5 copy-start.1
  213.8 3.5 copy-start.44
  270.9 270.4 %all-gather.19.cloned.1.call-start = ((), (), s32[]{:S(2)}) async-start(), calls=%async_computation.15 | async-start | bytes 15728640 | tf_op jit(solution)/shard_map/all_gather | solution.py:11
  400.1 3.0 copy-start.12
  400.1 3.0 copy-start.31
  403.2 3.1 copy-start.8
  407.2 4.3 copy-start.67
  408.9 5.5 copy-start.13
  411.5 4.1 copy-start.62
  418.7 194.7 %reduce-scatter.9.cloned.1.call-start = ((), (), s32[]{:S(2)}) async-start(), calls=%async_computation.8 | async-start | bytes 1179648 | tf_op jit(solution)/shard_map/reduce_scatter | solution.py:190
  548.7 8.1 copy-start.46
  548.7 8.1 copy-start.48
  548.7 8.1 copy-start.33
  548.7 8.2 copy-start.35
  548.7 11.1 %copy-start.19 = (bf16[192,768]{0,1:T(8,128)(2,1)S(1)}, bf16[192,768]{0,1:T(8,128)(2,1)}, u32[]{:S(2)}) copy-start(bf16[192,768]{0,1:T(8,128)(2,1)} %copy-done.18) | copy-start | bytes 884740
  556.9 2.9 copy-start.3
  556.9 4.0 copy-start.7
  556.9 4.9 copy-start.14
  556.9 4.9 copy-start.38
  564.2 31.7 %copy-start.4 = (f32[2,512,768]{2,1,0:T(8,128)S(1)}, f32[2,512,768]{2,1,0:T(8,128)}, u32[]{:S(2)}) copy-start(f32[2,512,768]{2,1,0:T(8,128)} %get-tuple-element.213) | copy-start | bytes 9437188
  594.9 20.2 %reduce-scatter.11.cloned.1.call-start = ((), (), s32[]{:S(2)}) async-start(), calls=%async_computation.9 | async-start | bytes 1179648 | tf_op jit(solution)/shard_map/reduce_scatter | solution.py:193
  595.6 43.9 %reduce-scatter.19.cloned.1.call-start = ((), (), s32[]{:S(2)}) async-start(), calls=%async_computation.17 | async-start | bytes 491520
  598.4 5.0 copy-start.39
  598.4 5.0 copy-start.41
  598.5 71.0 %reduce-scatter.17.cloned.1.call-start = ((), (), s32[]{:S(2)}) async-start(), calls=%async_computation.12 | async-start | bytes 1474560 | tf_op jit(solution)/shard_map/reduce_scatter | solution.py:226
  603.4 96.2 %reduce-scatter.15.cloned.1.call-start = ((), (), s32[]{:S(2)}) async-start(), calls=%async_computation.11 | async-start | bytes 1474560 | tf_op jit(solution)/shard_map/reduce_scatter | solution.py:223
  603.4 5.2 copy-start.2
  608.6 121.8 %reduce-scatter.13.cloned.1.call-start = ((), (), s32[]{:S(2)}) async-start(), calls=%async_computation.10 | async-start | bytes 1474560 | tf_op jit(solution)/shard_map/reduce_scatter | solution.py:217
  612.3 6.0 copy-start.22
  618.3 112.2 %copy-start.17 = (bf16[768,3,192]{2,0,1:T(8,128)(2,1)S(1)}, bf16[768,3,192]{2,0,1:T(8,128)(2,1)}, u32[]{:S(2)}) copy-start(bf16[768,3,192]{2,0,1:T(8,128)(2,1)} %copy-done.16) | copy-start | bytes 2654212
  622.1 129.5 %all-reduce.4.cloned.1.call-start = ((), (), s32[]{:S(2)}) async-start(), calls=%async_computation.18 | async-start | bytes 1966080 | tf_op jit(solution)/shard_map/psum | solution.py:231
  730.5 147.2 %all-gather.21.cloned.1.call-start = ((), (), s32[]{:S(2)}) async-start(), calls=%async_computation.16 | async-start | bytes 15728640 | tf_op jit(solution)/shard_map/all_gather | solution.py:11
  877.7 7.6 copy-start.5
  877.7 7.6 copy-start.43
  885.3 4.0 copy-start.60
  (39 other events, 59.8 us)
Sparse Core Ops, SparseCore 0:
  79.5 123.4 all-gather.14
  204.6 30.2 all-gather.10
  236.5 29.4 all-gather.12
  271.0 121.5 all-gather.16
  418.8 122.3 all-gather.18
  595.0 8.1 reduce-scatter.8
  605.4 9.2 reduce-scatter.10
  617.6 21.9 reduce-scatter.18
  641.9 27.5 reduce-scatter.16
  671.7 27.9 reduce-scatter.14
  702.5 27.9 reduce-scatter.12
  733.5 18.0 all-reduce.3
  754.0 123.6 all-gather.20
